TPU v7x, 32 devices: a whole 2x2x4 slice. The times are simulated.
32 devices in a mesh: tm: 8 (over y, x, core), mp: 4 (over z).
Axes of the slice: x: 2, y: 2, z: 4, core: 2. Of those that a mesh axis runs over, the one named last changes fastest.
Arguments:
- frames: bfloat16 [4096, 1024], P(('tm', 'mp')), may hold values from -6 to 6
- block_ids: int32 [4096], replicated, may hold values from 0 to 203, never falling along the last dimension, each value on 1 to 40 neighbouring positions
- valid_counts: int32 [8], replicated, may hold values from 1 to 512, as said below
- norm_attn: float32 [1024], replicated, may hold values from 0.25 to 1.75
- w_qkv: bfloat16 [1024, 3072], replicated, may hold values from -1 to 1
- w_attn_out: bfloat16 [1024, 1024], replicated, may hold values from -0.1875 to 0.1875
- norm_conv: float32 [1024], replicated, may hold values from 0.25 to 1.75
- w_point_in: bfloat16 [1024, 2048], replicated, may hold values from -0.1875 to 0.1875
- w_depth: bfloat16 [31, 1024], replicated, may hold values from -1 to 1
- w_point_out: bfloat16 [1024, 1024], replicated, may hold values from -0.1875 to 0.1875
- w_adapter: bfloat16 [1024, 8192], P('tm', 'mp'), may hold values from -1 to 1
- llm_gain: float32 [8192], replicated, may hold values from 0.25 to 1.75
- w_query: bfloat16 [8192, 8192], P('tm', 'mp'), may hold values from -1 to 1
- w_key: bfloat16 [8192, 1024], P('tm', 'mp'), may hold values from -1 to 1
- w_value: bfloat16 [8192, 1024], P('tm', 'mp'), may hold values from -0.0625 to 0.0625
Outputs:
- conf_out: bfloat16 [4096, 1024], P(('tm', 'mp'))
- attended: bfloat16 [1024, 8192], P('tm', 'mp')
Inputs may be any that keep to these rules, and one draw needn't show every extreme that they name: `block_ids`: block numbers never fall along the recording, and one block holds 1 to 40 frames. Every time shard but the last holds 512 real frames; the frames after the first valid_counts[t] of time shard t are padding.
All inputs are finite; a program needn't handle non-finite values.
Results may differ from a plain program's by a relative error of at most 0.014.
Values may be sent and summed in bfloat16 or wider, within the bound.
No kernel may reach another device: no remote copies, remote signals or barrier semaphores. Data moves between devices by JAX's collectives and lax.ppermute only.
A program may use at most 192 MiB of HBM per device.

v0:
```python
import math
import jax
import jax.numpy as jnp
from jax import lax
from jax.sharding import PartitionSpec as P

CH = 16
HDIM = 128
eps_conf = 1e-05
eps_llm = 1e-06
rope_base = 1000000.0
masked_score = -1e30


def passed_along(value, axis, by):
    length = lax.axis_size(axis)
    pairs = [(i, i + by) for i in range(length) if 0 <= i + by < length]
    return lax.ppermute(value, axis, pairs)


def shard_count(index, valid_counts, shard_len):
    shard = index // shard_len
    table = jnp.arange(valid_counts.shape[0], dtype=jnp.int32)
    hit = shard[:, None] == table[None, :]
    count = jnp.sum(jnp.where(hit, valid_counts[None, :], 0), axis=1)
    return (index - shard * shard_len, count)


def layer_norm(field, gain):
    center = field - jnp.mean(field, axis=-1, keepdims=True)
    spread = jnp.mean(center * center, axis=-1, keepdims=True)
    return center * lax.rsqrt(spread + eps_conf) * gain


def rotary(field, positions):
    half = field.shape[-1] // 2
    freq = rope_base ** (-(jnp.arange(half, dtype=jnp.float32) * 2.0) / field.shape[-1])
    angle = positions.astype(jnp.float32)[:, None] * freq[None, :]
    cosine = jnp.concatenate([jnp.cos(angle), jnp.cos(angle)], axis=-1)[:, None, :]
    sine = jnp.concatenate([jnp.sin(angle), jnp.sin(angle)], axis=-1)[:, None, :]
    turned = jnp.concatenate([-field[..., half:], field[..., :half]], axis=-1)
    return field * cosine + turned * sine


def on_device(
    frames,
    block_ids,
    valid_counts,
    norm_attn,
    w_qkv,
    w_attn_out,
    norm_conv,
    w_point_in,
    w_depth,
    w_point_out,
    w_adapter,
    llm_gain,
    w_query,
    w_key,
    w_value,
):
    mp_count = lax.axis_size("mp")
    frame_rows, width = frames.shape
    heads = CH
    head_size = width // heads
    shard_frames = frame_rows * mp_count
    time_place = lax.axis_index("tm")
    model_place = lax.axis_index("mp")
    first = (time_place * mp_count + model_place) * frame_rows
    inputs = frames.astype(jnp.float32)
    own_index = first + jnp.arange(frame_rows, dtype=jnp.int32)
    own_place, own_count = shard_count(own_index, valid_counts, shard_frames)
    frame_real = own_place < own_count
    normed = layer_norm(inputs, norm_attn).astype(jnp.bfloat16)
    projected = jnp.dot(normed, w_qkv, preferred_element_type=jnp.float32).astype(jnp.bfloat16)
    queries = projected[:, :width]
    own_keys = projected[:, width : 2 * width]
    own_values = projected[:, 2 * width :]
    prior_keys, prior_values = passed_along((own_keys, own_values), ("tm", "mp"), 1)
    keys = jnp.concatenate([prior_keys, own_keys], axis=0).reshape(2 * frame_rows, heads, head_size)
    values = jnp.concatenate([prior_values, own_values], axis=0).reshape(
        2 * frame_rows, heads, head_size
    )
    key_index = first - frame_rows + jnp.arange(2 * frame_rows, dtype=jnp.int32)
    key_place, key_count = shard_count(key_index, valid_counts, shard_frames)
    key_real = key_place < key_count
    prior_ids = lax.dynamic_slice_in_dim(
        block_ids, jnp.maximum(first - frame_rows, 0), frame_rows, 0
    )
    query_ids = lax.dynamic_slice_in_dim(block_ids, first, frame_rows, 0)
    key_ids = jnp.concatenate([prior_ids, query_ids], axis=0)
    same = key_index[None, :] == own_index[:, None]
    visible = (
        (key_index[None, :] <= own_index[:, None])
        & (key_ids[None, :] >= query_ids[:, None] - 2)
        & (key_real[None, :] | same)
    )
    query_heads = queries.reshape(frame_rows, heads, head_size)
    scores = jnp.einsum(
        "qhd,khd->hqk", query_heads, keys, preferred_element_type=jnp.float32
    ) / jnp.sqrt(jnp.float32(head_size))
    scores = jnp.where(visible[None], scores, masked_score)
    top = jnp.max(scores, axis=-1, keepdims=True)
    weights = jnp.where(visible[None], jnp.exp(scores - top), 0.0)
    total = jnp.sum(weights, axis=-1)
    summed = jnp.einsum(
        "hqk,khd->qhd", weights.astype(jnp.bfloat16), values, preferred_element_type=jnp.float32
    )
    conf_context = (
        (summed / jnp.transpose(total)[:, :, None]).reshape(frame_rows, width).astype(jnp.bfloat16)
    )
    mid = inputs + jnp.dot(conf_context, w_attn_out, preferred_element_type=jnp.float32)
    conv_in = layer_norm(mid, norm_conv).astype(jnp.bfloat16)
    both = jnp.dot(conv_in, w_point_in, preferred_element_type=jnp.float32)
    glu = both[:, :width] * jax.nn.sigmoid(both[:, width:])
    glu = jnp.where(frame_real[:, None], glu, 0.0).astype(jnp.bfloat16)
    taps = w_depth.shape[0]
    rim = passed_along(glu[frame_rows - (taps - 1) :], ("tm", "mp"), 1)
    padded = jnp.concatenate([rim, glu], axis=0).astype(jnp.float32)
    kernel = w_depth.astype(jnp.float32)
    depth = jnp.zeros((frame_rows, width), jnp.float32)
    for tap in range(taps):
        depth = depth + kernel[tap][None, :] * padded[taps - 1 - tap : taps - 1 - tap + frame_rows]
    activated = jax.nn.silu(depth).astype(jnp.bfloat16)
    final = mid + jnp.dot(activated, w_point_out, preferred_element_type=jnp.float32)
    conf_out = jnp.where(frame_real[:, None], final, 0.0).astype(jnp.bfloat16)
    pooled = (
        jnp.sum(conf_out.astype(jnp.float32).reshape(frame_rows // 4, 4, width), axis=1) * 0.25
    ).astype(jnp.bfloat16)
    shard_pooled = lax.all_gather(pooled, "mp", axis=0, tiled=True)
    shard_tokens = shard_pooled.shape[0]
    adapter_part = lax.all_gather(w_adapter, "tm", axis=0, tiled=True)
    adapter_full = lax.all_gather(adapter_part, "mp", axis=1, tiled=True)
    adapted = jnp.dot(shard_pooled, adapter_full, preferred_element_type=jnp.float32)
    llm_in = (
        adapted
        * lax.rsqrt(jnp.mean(adapted * adapted, axis=-1, keepdims=True) + eps_llm)
        * llm_gain
    ).astype(jnp.bfloat16)
    query_cols = w_query.shape[1]
    key_cols = w_key.shape[1]
    raw_query = jnp.dot(
        llm_in,
        lax.all_gather(w_query, "tm", axis=0, tiled=True),
        preferred_element_type=jnp.float32,
    )
    raw_keys = jnp.dot(
        llm_in, lax.all_gather(w_key, "tm", axis=0, tiled=True), preferred_element_type=jnp.float32
    )
    raw_values = jnp.dot(
        llm_in,
        lax.all_gather(w_value, "tm", axis=0, tiled=True),
        preferred_element_type=jnp.float32,
    )
    llm_size = HDIM
    query_heads_dev = query_cols // llm_size
    kv_heads = key_cols // llm_size
    group = query_heads_dev // kv_heads
    token_index = time_place * shard_tokens + jnp.arange(shard_tokens, dtype=jnp.int32)
    llm_query = rotary(
        raw_query.reshape(shard_tokens, query_heads_dev, llm_size), token_index
    ).astype(jnp.bfloat16)
    llm_query = llm_query.reshape(shard_tokens, kv_heads, group, llm_size)
    llm_keys = (
        rotary(raw_keys.reshape(shard_tokens, kv_heads, llm_size), token_index)
        .astype(jnp.bfloat16)
        .reshape(shard_tokens, key_cols)
    )
    llm_values = raw_values.astype(jnp.bfloat16)
    score_scale = 1.0 / jnp.sqrt(jnp.float32(llm_size))
    start_state = (
        jnp.full((kv_heads, group, shard_tokens), masked_score, jnp.float32),
        jnp.zeros((kv_heads, group, shard_tokens), jnp.float32),
        jnp.zeros((kv_heads, group, shard_tokens, llm_size), jnp.float32),
    )
    key_piece = lax.all_gather(llm_keys, "tm", axis=0, tiled=True)
    value_piece = lax.all_gather(llm_values, "tm", axis=0, tiled=True)
    piece_rows = key_piece.shape[0]
    step_rows = math.gcd(piece_rows, 512)

    def one_step(block, state):
        best, total_weight, accum = state
        key_block = lax.dynamic_slice_in_dim(key_piece, block * step_rows, step_rows, 0).reshape(
            step_rows, kv_heads, llm_size
        )
        value_block = lax.dynamic_slice_in_dim(
            value_piece, block * step_rows, step_rows, 0
        ).reshape(step_rows, kv_heads, llm_size)
        block_index = block * step_rows + jnp.arange(step_rows, dtype=jnp.int32)
        block_place, block_count = shard_count(block_index, valid_counts, shard_tokens)
        block_real = block_place * 4 < block_count
        matches = block_index[None, :] == token_index[:, None]
        seen = (block_index[None, :] <= token_index[:, None]) & (block_real[None, :] | matches)
        block_scores = (
            jnp.einsum("qhgd,khd->hgqk", llm_query, key_block, preferred_element_type=jnp.float32)
            * score_scale
        )
        block_scores = jnp.where(seen[None, None], block_scores, masked_score)
        new_best = jnp.maximum(best, jnp.max(block_scores, axis=-1))
        block_weights = jnp.where(
            seen[None, None], jnp.exp(block_scores - new_best[..., None]), 0.0
        )
        fade = jnp.exp(best - new_best)
        total_weight = total_weight * fade + jnp.sum(block_weights, axis=-1)
        accum = accum * fade[..., None] + jnp.einsum(
            "hgqk,khd->hgqd",
            block_weights.astype(jnp.bfloat16),
            value_block,
            preferred_element_type=jnp.float32,
        )
        return (new_best, total_weight, accum)

    best, total_weight, accum = lax.fori_loop(0, piece_rows // step_rows, one_step, start_state)
    result = accum / total_weight[..., None]
    attended = (
        jnp.transpose(result, (2, 0, 1, 3)).reshape(shard_tokens, query_cols).astype(jnp.bfloat16)
    )
    return (conf_out, attended)


def solution(mesh):
    placed = (
        P(("tm", "mp"), None),
        P(),
        P(),
        P(),
        P(),
        P(),
        P(),
        P(),
        P(),
        P(),
        P("tm", "mp"),
        P(),
        P("tm", "mp"),
        P("tm", "mp"),
        P("tm", "mp"),
    )
    return jax.shard_map(
        on_device,
        mesh=mesh,
        in_specs=placed,
        out_specs=(P(("tm", "mp"), None), P("tm", "mp")),
        check_vma=False,
    )
```

profile of v0, /device:TPU:0, one launch (start us, length us, event | category | flops | bytes accessed | tf_op | source)
XLA Modules:
  0.0 644.8 jit_solution(2328061743884182033)
XLA Ops:
  7.2 0.7 all-gather.6.cloned.1.call-update
  8.0 41.4 %all-gather.6.cloned.1.call-done = bf16[1024,2048]{1,0:T(8,128)(2,1)} async-done(((bf16[128,2048]{1,0:T(8,128)(2,1)}), bf16[1024,2048]{1,0:T(8,128)(2,1)}) %all-gather.6.cloned.1.call-update) | async-done | bytes 4194320 | tf_op jit(solution)/shard_map/all_gather | solution.py:132
  51.7 3.9 convolution_convert_fusion
  55.6 0.8 fusion.92
  56.3 3.4 collective-permute-start.1
  59.7 4.1 collective-permute-start
  63.9 0.9 broadcast_add_fusion
  64.9 0.7 or_and_fusion.1
  66.2 0.7 fusion.93
  67.3 0.8 copy.53
  69.6 10.4 %collective-permute-done = bf16[128,1024]{1,0:T(8,128)(2,1)} collective-permute-done((bf16[128,1024]{1,0:T(8,128)(2,1)}, bf16[128,1024]{1,0:T(8,128)(2,1)}, u32[]{:S(2)}, u32[]{:S(2)}) %collective-permute-start) | collective-permute-done | bytes 262176 | tf_op jit(solution)/shard_map/ppermute | solution.py:18
  80.0 1.1 pad_maximum_fusion
  81.1 1.0 copy.52
  82.1 2.0 fusion.95
  84.1 1.8 fusion.97
  86.0 3.9 fusion.22
  91.0 3.1 fusion.72
  94.3 13.2 %collective-permute-start.2 = (bf16[30,1024]{1,0:T(8,128)(2,1)S(1)}, bf16[30,1024]{1,0:T(8,128)(2,1)S(1)}, u32[]{:S(2)}, u32[]{:S(2)}) collective-permute-start(bf16[30,1024]{1,0:T(8,128)(2,1)S(1)} %slice.294), channel_id=1, source_target_pairs={{0,1},{1,2},{2,3},{3,4},{4,5},{5,6},{6,7},{7,8},{8,9},{9,10},{10,1... | collective-permute-start | bytes 184328 | tf_op jit(solution)/shard_map/ppermute | solution.py:18
  107.6 3.0 collective-permute-done.2
  111.1 2.5 fusion.23
  114.1 36.5 %all_gather.24 = bf16[128,1024]{1,0:T(8,128)(2,1)S(1)} all-gather(bf16[32,1024]{1,0:T(8,128)(2,1)S(1)} %multiply_convert_fusion.5), channel_id=1, replica_groups=mesh['tm'=8,'mp'=4] {'mp'}, dimensions={0}, use_global_device_ids=true | all-gather | bytes 327680 | tf_op jit(solution)/shard_map/all_gather | solution.py:130
  150.6 200.2 %all-gather.8.cloned.1.call-done = bf16[1024,8192]{1,0:T(8,128)(2,1)} async-done(((bf16[1024,2048]{1,0:T(8,128)(2,1)}), bf16[1024,8192]{1,0:T(8,128)(2,1)}) %all-gather.8.cloned.1.call-update) | async-done | bytes 16777232 | tf_op jit(solution)/shard_map/all_gather | solution.py:133
  350.8 8.2 %multiply_reduce_fusion = (f32[128]{0:T(128)S(1)}, f32[128,8192]{1,0:T(8,128)S(1)}) fusion(bf16[128,1024]{1,0:T(8,128)(2,1)S(1)} %all_gather.24, bf16[1024,8192]{1,0:T(8,128)(2,1)} %all-gather.8.cloned.1.call-done), kind=kOutput, calls=%fused_computation.35 | convolution fusion | flops 2149580800 | bytes 21234176 | tf_op jit(solution)/shard_map/dot_general | solution.py:134
  359.5 27.4 %all-gather.10.cloned.1.call-done = bf16[8192,256]{1,0:T(8,128)(2,1)} async-done(((bf16[1024,256]{1,0:T(8,128)(2,1)}), bf16[8192,256]{1,0:T(8,128)(2,1)}) %all-gather.10.cloned.1.call-update) | async-done | bytes 4194320 | tf_op jit(solution)/shard_map/all_gather | solution.py:148
  386.9 2.9 fusion.98
  390.4 12.2 %all_gather.28 = bf16[1024,256]{1,0:T(8,128)(2,1)} all-gather(bf16[128,256]{1,0:T(8,128)(2,1)S(1)} %fusion.82), channel_id=1, replica_groups=mesh['tm'=8,'mp'=4] {'tm'}, dimensions={0}, use_global_device_ids=true | all-gather | bytes 589824 | tf_op jit(solution)/shard_map/all_gather | solution.py:176
  402.6 23.5 %all-gather.14.cloned.1.call-done = bf16[8192,256]{1,0:T(8,128)(2,1)} async-done(((bf16[1024,256]{1,0:T(8,128)(2,1)}), bf16[8192,256]{1,0:T(8,128)(2,1)}) %all-gather.14.cloned.1.call-update) | async-done | bytes 4194320 | tf_op jit(solution)/shard_map/all_gather | solution.py:152
  426.1 2.9 convolution_convert_fusion.1
  429.0 10.8 %all_gather.31 = bf16[1024,256]{1,0:T(8,128)(2,1)} all-gather(bf16[128,256]{1,0:T(8,128)(2,1)S(1)} %convolution_convert_fusion.1), channel_id=1, replica_groups=mesh['tm'=8,'mp'=4] {'tm'}, dimensions={0}, use_global_device_ids=true | all-gather | bytes 589824 | tf_op jit(solution)/shard_map/all_gather | solution.py:177
  439.8 148.9 %all-gather.12.cloned.1.call-done = bf16[8192,2048]{1,0:T(8,128)(2,1)} async-done(((bf16[1024,2048]{1,0:T(8,128)(2,1)}), bf16[8192,2048]{1,0:T(8,128)(2,1)}) %all-gather.12.cloned.1.call-update) | async-done | bytes 33554448 | tf_op jit(solution)/shard_map/all_gather | solution.py:144
  588.7 12.9 %fusion.99 = f32[128,2048]{1,0:T(8,128)S(1)} fusion(bf16[128,8192]{1,0:T(8,128)(2,1)S(1)} %multiply_convert_fusion, bf16[8192,2048]{1,0:T(8,128)(2,1)} %all-gather.12.cloned.1.call-done), kind=kOutput, calls=%fused_computation.199 | convolution fusion | flops 4294967296 | bytes 36700160 | tf_op jit(solution)/shard_map/dot_general | solution.py:142
  601.9 1.1 slice_negate_fusion
  603.0 2.4 copy.57
  605.4 2.4 copy.58
  608.0 2.2 fusion.25
  610.2 25.0 %while.20 = (s32[]{:T(128)}, f32[2,8,128]{2,1,0:T(8,128)S(1)}, f32[2,8,128]{2,1,0:T(8,128)S(1)}, f32[2,8,128,128]{3,2,1,0:T(8,128)}, s32[8]{0:T(128)S(1)}, /*ind...) while((s32[]{:T(128)}, f32[2,8,128]{2,1,0:T(8,128)S(1)}, ...), condition=%wide.region_14.15_spmd.clone, body=%wide.region_10.14_spmd.clone.sunk | while | flops 551591552 | bytes 26622240 | solution.py:213
  610.6 1.0 constant_dynamic-slice_fusion.3
  611.7 2.8 fusion.133
  614.6 3.2 fusion.134
  617.9 3.9 fusion.136
  621.8 0.9 copy-done.5
  623.1 1.0 constant_dynamic-slice_fusion.3
  624.3 2.8 fusion.133
  627.1 3.2 fusion.134
  630.4 3.9 fusion.136
  634.3 0.9 copy-done.5
  635.3 1.7 fusion.70
  637.4 0.9 copy.81
  (168 shorter events, 9.9 us)
Async XLA Ops:
  7.2 82.7 %copy-start = (bf16[1024,1024]{1,0:T(8,128)(2,1)S(1)}, bf16[1024,1024]{1,0:T(8,128)(2,1)}, u32[]{:S(2)}) copy-start(bf16[1024,1024]{1,0:T(8,128)(2,1)} %param.22) | copy-start | bytes 6291460
  7.2 42.2 %all-gather.6.cloned.1.call-start = ((), (), s32[]{:S(2)}) async-start(), calls=%async_computation | async-start | bytes 4718592 | tf_op jit(solution)/shard_map/all_gather | solution.py:132
  7.9 342.8 %all-gather.8.cloned.1.call-start = ((), (), s32[]{:S(2)}) async-start(), calls=%async_computation.1 | async-start | bytes 20971520 | tf_op jit(solution)/shard_map/all_gather | solution.py:133
  49.4 337.5 %all-gather.10.cloned.1.call-start = ((), (), s32[]{:S(2)}) async-start(), calls=%async_computation.2 | async-start | bytes 4718592 | tf_op jit(solution)/shard_map/all_gather | solution.py:148
  50.1 376.0 %all-gather.14.cloned.1.call-start = ((), (), s32[]{:S(2)}) async-start(), calls=%async_computation.4 | async-start | bytes 4718592 | tf_op jit(solution)/shard_map/all_gather | solution.py:152
  50.7 538.0 %all-gather.12.cloned.1.call-start = ((), (), s32[]{:S(2)}) async-start(), calls=%async_computation.3 | async-start | bytes 37748736 | tf_op jit(solution)/shard_map/all_gather | solution.py:144
  51.7 13.1 %copy-start.11 = (s32[8]{0:T(128)S(1)}, s32[8]{0:T(128)}, u32[]{:S(2)}) copy-start(s32[8]{0:T(128)} %param.19) | copy-start | bytes 100
  51.7 13.9 %copy-start.8 = (bf16[31,1024]{1,0:T(8,128)(2,1)S(1)}, bf16[31,1024]{1,0:T(8,128)(2,1)}, u32[]{:S(2)}) copy-start(bf16[31,1024]{1,0:T(8,128)(2,1)} %param.25) | copy-start | bytes 190468
  56.3 13.0 %collective-permute-start.1 = (bf16[128,1024]{1,0:T(8,128)(2,1)S(1)}, bf16[128,1024]{1,0:T(8,128)(2,1)S(1)}, u32[]{:S(2)}, u32[]{:S(2)}) collective-permute-start(bf16[128,1024]{1,0:T(8,128)(2,1)S(1)} %get-tuple-element.316), channel_id=1, source_target_pairs={{0,1},{1,2},{2,3},{3,4},{4,5},{5,6},{6,7},{7,8},{8,9},{9,10},{10,1... | collective-permute-start | bytes 786440 | tf_op jit(solution)/shard_map/ppermute | solution.py:18
  59.7 20.3 %collective-permute-start = (bf16[128,1024]{1,0:T(8,128)(2,1)}, bf16[128,1024]{1,0:T(8,128)(2,1)}, u32[]{:S(2)}, u32[]{:S(2)}) collective-permute-start(bf16[128,1024]{1,0:T(8,128)(2,1)} %get-tuple-element.318), channel_id=1, source_target_pairs={{0,1},{1,2},{2,3},{3,4},{4,5},{5,6},{6,7},{7,8},{8,9},{9,10},{10,1... | collective-permute-start | bytes 786440 | tf_op jit(solution)/shard_map/ppermute | solution.py:18
  90.6 20.1 %copy-start.13 = (f32[1,1024]{1,0:T(1,128)S(1)}, f32[1,1024]{1,0:T(1,128)}, u32[]{:S(2)}) copy-start(f32[1,1024]{1,0:T(1,128)} %get-tuple-element.340) | copy-start | bytes 12292
  90.7 20.1 %copy-start.14 = (f32[1,1024]{1,0:T(1,128)S(1)}, f32[1,1024]{1,0:T(1,128)}, u32[]{:S(2)}) copy-start(f32[1,1024]{1,0:T(1,128)} %get-tuple-element.341) | copy-start | bytes 12292
  90.7 20.1 %copy-start.15 = (f32[1,1024]{1,0:T(1,128)S(1)}, f32[1,1024]{1,0:T(1,128)}, u32[]{:S(2)}) copy-start(f32[1,1024]{1,0:T(1,128)} %get-tuple-element.342) | copy-start | bytes 12292
  90.7 20.1 %copy-start.16 = (f32[1,1024]{1,0:T(1,128)S(1)}, f32[1,1024]{1,0:T(1,128)}, u32[]{:S(2)}) copy-start(f32[1,1024]{1,0:T(1,128)} %get-tuple-element.343) | copy-start | bytes 12292
  90.7 20.1 %copy-start.17 = (f32[1,1024]{1,0:T(1,128)S(1)}, f32[1,1024]{1,0:T(1,128)}, u32[]{:S(2)}) copy-start(f32[1,1024]{1,0:T(1,128)} %get-tuple-element.344) | copy-start | bytes 12292
  90.7 20.1 %copy-start.18 = (f32[1,1024]{1,0:T(1,128)S(1)}, f32[1,1024]{1,0:T(1,128)}, u32[]{:S(2)}) copy-start(f32[1,1024]{1,0:T(1,128)} %get-tuple-element.345) | copy-start | bytes 12292
  90.7 20.1 %copy-start.19 = (f32[1,1024]{1,0:T(1,128)S(1)}, f32[1,1024]{1,0:T(1,128)}, u32[]{:S(2)}) copy-start(f32[1,1024]{1,0:T(1,128)} %get-tuple-element.346) | copy-start | bytes 12292
  90.7 20.1 %copy-start.20 = (f32[1,1024]{1,0:T(1,128)S(1)}, f32[1,1024]{1,0:T(1,128)}, u32[]{:S(2)}) copy-start(f32[1,1024]{1,0:T(1,128)} %get-tuple-element.347) | copy-start | bytes 12292
  90.7 20.1 %copy-start.21 = (f32[1,1024]{1,0:T(1,128)S(1)}, f32[1,1024]{1,0:T(1,128)}, u32[]{:S(2)}) copy-start(f32[1,1024]{1,0:T(1,128)} %get-tuple-element.348) | copy-start | bytes 12292
  90.7 20.1 %copy-start.22 = (f32[1,1024]{1,0:T(1,128)S(1)}, f32[1,1024]{1,0:T(1,128)}, u32[]{:S(2)}) copy-start(f32[1,1024]{1,0:T(1,128)} %get-tuple-element.349) | copy-start | bytes 12292
  90.7 20.1 %copy-start.23 = (f32[1,1024]{1,0:T(1,128)S(1)}, f32[1,1024]{1,0:T(1,128)}, u32[]{:S(2)}) copy-start(f32[1,1024]{1,0:T(1,128)} %get-tuple-element.350) | copy-start | bytes 12292
  90.8 20.1 %copy-start.24 = (f32[1,1024]{1,0:T(1,128)S(1)}, f32[1,1024]{1,0:T(1,128)}, u32[]{:S(2)}) copy-start(f32[1,1024]{1,0:T(1,128)} %get-tuple-element.351) | copy-start | bytes 12292
  90.8 20.1 %copy-start.25 = (f32[1,1024]{1,0:T(1,128)S(1)}, f32[1,1024]{1,0:T(1,128)}, u32[]{:S(2)}) copy-start(f32[1,1024]{1,0:T(1,128)} %get-tuple-element.321) | copy-start | bytes 12292
  90.8 20.1 %copy-start.26 = (f32[1,1024]{1,0:T(1,128)S(1)}, f32[1,1024]{1,0:T(1,128)}, u32[]{:S(2)}) copy-start(f32[1,1024]{1,0:T(1,128)} %get-tuple-element.322) | copy-start | bytes 12292
  90.8 20.1 %copy-start.27 = (f32[1,1024]{1,0:T(1,128)S(1)}, f32[1,1024]{1,0:T(1,128)}, u32[]{:S(2)}) copy-start(f32[1,1024]{1,0:T(1,128)} %get-tuple-element.323) | copy-start | bytes 12292
  90.8 20.1 %copy-start.28 = (f32[1,1024]{1,0:T(1,128)S(1)}, f32[1,1024]{1,0:T(1,128)}, u32[]{:S(2)}) copy-start(f32[1,1024]{1,0:T(1,128)} %get-tuple-element.324) | copy-start | bytes 12292
  90.8 20.1 %copy-start.29 = (f32[1,1024]{1,0:T(1,128)S(1)}, f32[1,1024]{1,0:T(1,128)}, u32[]{:S(2)}) copy-start(f32[1,1024]{1,0:T(1,128)} %get-tuple-element.325) | copy-start | bytes 12292
  90.8 20.1 %copy-start.30 = (f32[1,1024]{1,0:T(1,128)S(1)}, f32[1,1024]{1,0:T(1,128)}, u32[]{:S(2)}) copy-start(f32[1,1024]{1,0:T(1,128)} %get-tuple-element.326) | copy-start | bytes 12292
  90.8 20.1 %copy-start.31 = (f32[1,1024]{1,0:T(1,128)S(1)}, f32[1,1024]{1,0:T(1,128)}, u32[]{:S(2)}) copy-start(f32[1,1024]{1,0:T(1,128)} %get-tuple-element.327) | copy-start | bytes 12292
  90.8 20.1 %copy-start.32 = (f32[1,1024]{1,0:T(1,128)S(1)}, f32[1,1024]{1,0:T(1,128)}, u32[]{:S(2)}) copy-start(f32[1,1024]{1,0:T(1,128)} %get-tuple-element.328) | copy-start | bytes 12292
  90.8 20.1 %copy-start.33 = (f32[1,1024]{1,0:T(1,128)S(1)}, f32[1,1024]{1,0:T(1,128)}, u32[]{:S(2)}) copy-start(f32[1,1024]{1,0:T(1,128)} %get-tuple-element.329) | copy-start | bytes 12292
  90.9 20.1 %copy-start.34 = (f32[1,1024]{1,0:T(1,128)S(1)}, f32[1,1024]{1,0:T(1,128)}, u32[]{:S(2)}) copy-start(f32[1,1024]{1,0:T(1,128)} %get-tuple-element.330) | copy-start | bytes 12292
  90.9 20.1 %copy-start.35 = (f32[1,1024]{1,0:T(1,128)S(1)}, f32[1,1024]{1,0:T(1,128)}, u32[]{:S(2)}) copy-start(f32[1,1024]{1,0:T(1,128)} %get-tuple-element.331) | copy-start | bytes 12292
  90.9 20.1 %copy-start.36 = (f32[1,1024]{1,0:T(1,128)S(1)}, f32[1,1024]{1,0:T(1,128)}, u32[]{:S(2)}) copy-start(f32[1,1024]{1,0:T(1,128)} %get-tuple-element.332) | copy-start | bytes 12292
  90.9 20.1 %copy-start.37 = (f32[1,1024]{1,0:T(1,128)S(1)}, f32[1,1024]{1,0:T(1,128)}, u32[]{:S(2)}) copy-start(f32[1,1024]{1,0:T(1,128)} %get-tuple-element.333) | copy-start | bytes 12292
  90.9 20.1 %copy-start.38 = (f32[1,1024]{1,0:T(1,128)S(1)}, f32[1,1024]{1,0:T(1,128)}, u32[]{:S(2)}) copy-start(f32[1,1024]{1,0:T(1,128)} %get-tuple-element.334) | copy-start | bytes 12292
  90.9 20.1 %copy-start.39 = (f32[1,1024]{1,0:T(1,128)S(1)}, f32[1,1024]{1,0:T(1,128)}, u32[]{:S(2)}) copy-start(f32[1,1024]{1,0:T(1,128)} %get-tuple-element.335) | copy-start | bytes 12292
  90.9 20.1 %copy-start.40 = (f32[1,1024]{1,0:T(1,128)S(1)}, f32[1,1024]{1,0:T(1,128)}, u32[]{:S(2)}) copy-start(f32[1,1024]{1,0:T(1,128)} %get-tuple-element.336) | copy-start | bytes 12292
  90.9 20.1 %copy-start.41 = (f32[1,1024]{1,0:T(1,128)S(1)}, f32[1,1024]{1,0:T(1,128)}, u32[]{:S(2)}) copy-start(f32[1,1024]{1,0:T(1,128)} %get-tuple-element.337) | copy-start | bytes 12292
  90.9 20.1 %copy-start.42 = (f32[1,1024]{1,0:T(1,128)S(1)}, f32[1,1024]{1,0:T(1,128)}, u32[]{:S(2)}) copy-start(f32[1,1024]{1,0:T(1,128)} %get-tuple-element.338) | copy-start | bytes 12292
  90.9 20.1 %copy-start.43 = (f32[1,1024]{1,0:T(1,128)S(1)}, f32[1,1024]{1,0:T(1,128)}, u32[]{:S(2)}) copy-start(f32[1,1024]{1,0:T(1,128)} %get-tuple-element.339) | copy-start | bytes 12292
  91.0 20.1 %copy-start.46 = (bf16[1024,1024]{1,0:T(8,128)(2,1)S(1)}, bf16[1024,1024]{1,0:T(8,128)(2,1)}, u32[]{:S(2)}) copy-start(bf16[1024,1024]{1,0:T(8,128)(2,1)} %param.26) | copy-start | bytes 6291460
  94.3 16.3 %collective-permute-start.2 = (bf16[30,1024]{1,0:T(8,128)(2,1)S(1)}, bf16[30,1024]{1,0:T(8,128)(2,1)S(1)}, u32[]{:S(2)}, u32[]{:S(2)}) collective-permute-start(bf16[30,1024]{1,0:T(8,128)(2,1)S(1)} %slice.294), channel_id=1, source_target_pairs={{0,1},{1,2},{2,3},{3,4},{4,5},{5,6},{6,7},{7,8},{8,9},{9,10},{10,1... | collective-permute-start | bytes 184328 | tf_op jit(solution)/shard_map/ppermute | solution.py:18
  113.6 245.4 %copy-start.7 = (bf16[128,1024]{1,0:T(8,128)(2,1)}, bf16[128,1024]{1,0:T(8,128)(2,1)S(1)}, u32[]{:S(2)}) copy-start(bf16[128,1024]{1,0:T(8,128)(2,1)S(1)} %fusion.23) | copy-start | bytes 786436
  150.6 208.4 %copy-start.10 = (f32[8192]{0:T(1024)S(1)}, f32[8192]{0:T(1024)}, u32[]{:S(2)}) copy-start(f32[8192]{0:T(1024)} %param.28) | copy-start | bytes 98308
  603.0 7.2 %copy-start.2 = (bf16[1024,256]{1,0:T(8,128)(2,1)S(1)}, bf16[1024,256]{1,0:T(8,128)(2,1)}, u32[]{:S(2)}) copy-start(bf16[1024,256]{1,0:T(8,128)(2,1)} %all_gather.28) | copy-start | bytes 1572868
  603.0 7.2 %copy-start.12 = (s32[8]{0:T(128)S(1)}, s32[8]{0:T(128)}, u32[]{:S(2)}) copy-start(s32[8]{0:T(128)} %param.19) | copy-start | bytes 100
  624.2 6.2 copy-start.4
  (9 other events, 26.3 us)
Sparse Core Ops, SparseCore 0:
  9.9 39.4 all-gather.5
  50.9 299.7 all-gather.7
  352.7 34.2 all-gather.9
  388.7 37.3 all-gather.13
  427.8 160.7 all-gather.11
where the time goes:
time: 646 us; the launch traced here: 645 us
  waiting for transfers between devices  458 us (71%)
  blocking collectives  59.4 us (9%)
  matrix products  58.1 us (9%)
  starting transfers between devices  20.9 us (3%)
  other arithmetic  18.1 us (3%)
  local copies, waits for them, and re-layouts  15.7 us (2%)
  between operations  14.7 us (2%)
    all_gather x1, waiting for transfers between devices, on_device(): adapter_full = lax.all_gather(adapter_part, 'mp', axis=1, tiled=True)  200 us
    all_gather x1, waiting for transfers between devices, on_device(): lax.all_gather(w_query, 'tm', axis=0, tiled=True)  149 us
    all_gather x1, waiting for transfers between devices, on_device(): adapter_part = lax.all_gather(w_adapter, 'tm', axis=0, tiled=True)  41.4 us
    all_gather x1, blocking collectives, on_device(): shard_pooled = lax.all_gather(pooled, 'mp', axis=0, tiled=True)  36.5 us
    all_gather x1, waiting for transfers between devices, on_device(): lax.all_gather(w_key, 'tm', axis=0, tiled=True)  27.4 us
    all_gather x1, waiting for transfers between devices, on_device(): lax.all_gather(w_value, 'tm', axis=0, tiled=True)  23.5 us
    ppermute x3, starting transfers between devices, passed_along(): return lax.ppermute(value, axis, pairs)  20.7 us
    ppermute x3, waiting for transfers between devices, passed_along(): return lax.ppermute(value, axis, pairs)  14.1 us
  transfers between devices with their start and end apart: 8, of which 8 were waited for; matrix products, arithmetic and copies ran while one was open for 7% of the time, Pallas kernels for 0%

commit v1 on v0

--- a/solution.py
+++ b/solution.py
@@ -10,6 +10,19 @@
 eps_llm = 1e-06
 rope_base = 1000000.0
 masked_score = -1e30
+
+
+def ring_gather(x, axis, dim):
+    ways = lax.axis_size(axis)
+    up = [(d, (d + 1) % ways) for d in range(ways)]
+    down = [(d, (d - 1) % ways) for d in range(ways)]
+    earlier, later = ([x], [x])
+    for _ in range(ways // 2):
+        earlier.append(lax.ppermute(earlier[-1], axis, up))
+    for _ in range((ways - 1) // 2):
+        later.append(lax.ppermute(later[-1], axis, down))
+    line = jnp.concatenate([*earlier[::-1], *later[1:]], axis=dim)
+    return jnp.roll(line, (lax.axis_index(axis) - ways // 2) * x.shape[dim], axis=dim)
 
 
 def passed_along(value, axis, by):
@@ -147,11 +160,7 @@
     raw_keys = jnp.dot(
         llm_in, lax.all_gather(w_key, "tm", axis=0, tiled=True), preferred_element_type=jnp.float32
     )
-    raw_values = jnp.dot(
-        llm_in,
-        lax.all_gather(w_value, "tm", axis=0, tiled=True),
-        preferred_element_type=jnp.float32,
-    )
+    raw_values = jnp.dot(llm_in, ring_gather(w_value, "tm", 0), preferred_element_type=jnp.float32)
     llm_size = HDIM
     query_heads_dev = query_cols // llm_size
     kv_heads = key_cols // llm_size

time: 646 us -> 610 us (0.944)
  waiting for transfers between devices: 458 us -> 387 us
  local copies, waits for them, and re-layouts: 15.7 us -> 36.8 us
  starting transfers between devices: 20.9 us -> 28.7 us
    all_gather x1, waiting for transfers between devices: 200 us -> 164 us  [on_device(): adapter_full = lax.all_gather(adapter_part, 'mp', axis=1, tiled=True)]
    all_gather x1 -> x0, waiting for transfers between devices: 23.5 us -> none  [on_device(): lax.all_gather(w_value, 'tm', axis=0, tiled=True)]
    unnamed x92 -> x111, local copies, waits for them, and re-layouts: 1.32 us -> 16.7 us
    all_gather x1, waiting for transfers between devices: 149 us -> 135 us  [on_device(): lax.all_gather(w_query, 'tm', axis=0, tiled=True)]
    ppermute x0 -> x7, starting transfers between devices: none -> 8.44 us  [the longest x3 4.36 us: ring_gather(): later.append(lax.ppermute(later[-1], axis, down))]
    ppermute x0 -> x7, waiting for transfers between devices: none -> 6.82 us  [the longest x4 6.81 us: ring_gather(): earlier.append(lax.ppermute(earlier[-1], axis, up))]
  transfers between devices with their start and end apart: 8 -> 14, of which waited for: 8 -> 8; matrix products, arithmetic and copies ran while one was open for 7% -> 11% of each run, Pallas kernels for 0% -> 0%
where the time goes in v1:
time: 610 us; the launch traced here: 609 us
  waiting for transfers between devices  387 us (63%)
  matrix products  61.5 us (10%)
  blocking collectives  59.2 us (10%)
  local copies, waits for them, and re-layouts  36.8 us (6%)
  starting transfers between devices  28.7 us (5%)
  other arithmetic  21.2 us (3%)
  between operations  14.6 us (2%)
    all_gather x1, waiting for transfers between devices, on_device(): adapter_full = lax.all_gather(adapter_part, 'mp', axis=1, tiled=True)  164 us
    all_gather x1, waiting for transfers between devices, on_device(): lax.all_gather(w_query, 'tm', axis=0, tiled=True)  135 us
    all_gather x1, waiting for transfers between devices, on_device(): adapter_part = lax.all_gather(w_adapter, 'tm', axis=0, tiled=True)  41.4 us
    all_gather x1, blocking collectives, on_device(): shard_pooled = lax.all_gather(pooled, 'mp', axis=0, tiled=True)  35.6 us
    all_gather x1, waiting for transfers between devices, on_device(): lax.all_gather(w_key, 'tm', axis=0, tiled=True)  26.3 us
    ppermute x3, starting transfers between devices, passed_along(): return lax.ppermute(value, axis, pairs)  20.1 us
    unnamed x111, local copies, waits for them, and re-layouts  16.7 us
    dot_general x1, matrix products, on_device(): jnp.dot(llm_in, lax.all_gather(w_query, 'tm', axis=0, tiled=True), prefer...  12.9 us
  transfers between devices with their start and end apart: 14, of which 8 were waited for; matrix products, arithmetic and copies ran while one was open for 11% of the time, Pallas kernels for 0%

profile of v1, /device:TPU:0, one launch (start us, length us, event | category | flops | bytes accessed | tf_op | source)
XLA Modules:
  0.0 608.9 jit_solution(1272519139698077526)
XLA Ops:
  8.0 41.4 %all-gather.5.cloned.1.call-done = bf16[1024,2048]{1,0:T(8,128)(2,1)} async-done(((bf16[128,2048]{1,0:T(8,128)(2,1)}), bf16[1024,2048]{1,0:T(8,128)(2,1)}) %all-gather.5.cloned.1.call-update) | async-done | bytes 4194320 | tf_op jit(solution)/shard_map/all_gather | solution.py:145
  51.0 2.4 collective-permute-start.7
  53.8 3.9 convolution_convert_fusion
  58.6 4.1 collective-permute-start.1
  62.7 3.4 collective-permute-start
  69.7 1.8 copy.53
  71.5 3.1 collective-permute-done.1
  74.6 1.9 pad_maximum_fusion.1
  76.5 2.0 copy.54
  78.5 5.3 collective-permute-done
  83.8 1.9 pad_maximum_fusion
  85.6 2.1 copy.52
  87.7 2.1 fusion.101
  89.8 3.0 fusion.103
  92.8 4.5 fusion.24
  97.3 1.5 fusion.102
  98.8 2.4 collective-permute-start.4
  101.8 6.8 %collective-permute-done.4 = bf16[1024,256]{1,0:T(8,128)(2,1)S(1)} collective-permute-done((bf16[1024,256]{1,0:T(8,128)(2,1)}, bf16[1024,256]{1,0:T(8,128)(2,1)S(1)}, u32[]{:S(2)}, u32[]{:S(2)}) %collective-permute-start.4) | collective-permute-done | bytes 524320 | tf_op jit(solution)/shard_map/ppermute | solution.py:21
  109.2 3.0 fusion.77
  112.4 12.6 %collective-permute-start.2 = (bf16[30,1024]{1,0:T(8,128)(2,1)S(1)}, bf16[30,1024]{1,0:T(8,128)(2,1)S(1)}, u32[]{:S(2)}, u32[]{:S(2)}) collective-permute-start(bf16[30,1024]{1,0:T(8,128)(2,1)S(1)} %slice.294), channel_id=1, source_target_pairs={{0,1},{1,2},{2,3},{3,4},{4,5},{5,6},{6,7},{7,8},{8,9},{9,10},{10,1... | collective-permute-start | bytes 184328 | tf_op jit(solution)/shard_map/ppermute | solution.py:31
  125.1 3.2 collective-permute-done.2
  128.4 2.0 collective-permute-start.8
  131.4 3.1 fusion.25
  136.3 1.4 reduce_sum.120
  137.7 35.6 %all_gather.21 = bf16[128,1024]{1,0:T(8,128)(2,1)S(1)} all-gather(bf16[32,1024]{1,0:T(8,128)(2,1)S(1)} %multiply_convert_fusion.5), channel_id=1, replica_groups=mesh['tm'=8,'mp'=4] {'mp'}, dimensions={0}, use_global_device_ids=true | all-gather | bytes 327680 | tf_op jit(solution)/shard_map/all_gather | solution.py:143
  175.8 1.9 constant_dynamic-update-slice_fusion.12
  183.5 1.9 constant_dynamic-update-slice_fusion.4
  188.8 164.0 %all-gather.7.cloned.1.call-done = bf16[1024,8192]{1,0:T(8,128)(2,1)} async-done(((bf16[1024,2048]{1,0:T(8,128)(2,1)}), bf16[1024,8192]{1,0:T(8,128)(2,1)}) %all-gather.7.cloned.1.call-update) | async-done | bytes 16777232 | tf_op jit(solution)/shard_map/all_gather | solution.py:146
  352.8 8.4 %multiply_reduce_fusion = (f32[128]{0:T(128)S(1)}, f32[128,8192]{1,0:T(8,128)S(1)}) fusion(bf16[128,1024]{1,0:T(8,128)(2,1)S(1)} %all_gather.21, bf16[1024,8192]{1,0:T(8,128)(2,1)} %all-gather.7.cloned.1.call-done), kind=kOutput, calls=%fused_computation.37 | convolution fusion | flops 2149580800 | bytes 21234176 | tf_op jit(solution)/shard_map/dot_general | solution.py:147
  361.7 26.3 %all-gather.9.cloned.1.call-done = bf16[8192,256]{1,0:T(8,128)(2,1)} async-done(((bf16[1024,256]{1,0:T(8,128)(2,1)}), bf16[8192,256]{1,0:T(8,128)(2,1)}) %all-gather.9.cloned.1.call-update) | async-done | bytes 4194320 | tf_op jit(solution)/shard_map/all_gather | solution.py:161
  388.0 2.9 fusion.104
  391.0 2.9 fusion.26
  393.9 10.8 %all_gather.27 = bf16[1024,256]{1,0:T(8,128)(2,1)} all-gather(bf16[128,256]{1,0:T(8,128)(2,1)S(1)} %fusion.26), channel_id=1, replica_groups=mesh['tm'=8,'mp'=4] {'tm'}, dimensions={0}, use_global_device_ids=true | all-gather | bytes 589824 | tf_op jit(solution)/shard_map/all_gather | solution.py:186
  405.2 12.8 %all_gather.25 = bf16[1024,256]{1,0:T(8,128)(2,1)} all-gather(bf16[128,256]{1,0:T(8,128)(2,1)S(1)} %fusion.87), channel_id=1, replica_groups=mesh['tm'=8,'mp'=4] {'tm'}, dimensions={0}, use_global_device_ids=true | all-gather | bytes 589824 | tf_op jit(solution)/shard_map/all_gather | solution.py:185
  418.0 134.7 %all-gather.11.cloned.1.call-done = bf16[8192,2048]{1,0:T(8,128)(2,1)} async-done(((bf16[1024,2048]{1,0:T(8,128)(2,1)}), bf16[8192,2048]{1,0:T(8,128)(2,1)}) %all-gather.11.cloned.1.call-update) | async-done | bytes 33554448 | tf_op jit(solution)/shard_map/all_gather | solution.py:157
  552.7 12.9 %fusion.105 = f32[128,2048]{1,0:T(8,128)S(1)} fusion(bf16[128,8192]{1,0:T(8,128)(2,1)S(1)} %multiply_convert_fusion, bf16[8192,2048]{1,0:T(8,128)(2,1)} %all-gather.11.cloned.1.call-done), kind=kOutput, calls=%fused_computation.218 | convolution fusion | flops 4294967296 | bytes 36700160 | tf_op jit(solution)/shard_map/dot_general | solution.py:155
  565.9 1.1 slice_negate_fusion
  567.0 2.4 copy.57
  569.4 2.4 copy.58
  572.0 2.2 fusion.30
  574.3 25.1 %while.20 = (s32[]{:T(128)}, f32[2,8,128]{2,1,0:T(8,128)S(1)}, f32[2,8,128]{2,1,0:T(8,128)S(1)}, f32[2,8,128,128]{3,2,1,0:T(8,128)}, s32[8]{0:T(128)S(1)}, /*ind...) while((s32[]{:T(128)}, f32[2,8,128]{2,1,0:T(8,128)S(1)}, ...), condition=%wide.region_14.15_spmd.clone, body=%wide.region_10.14_spmd.clone.sunk | while | flops 551591552 | bytes 26622240 | solution.py:222
  575.8 2.8 fusion.138
  578.6 3.2 fusion.139
  582.0 3.9 fusion.141
  588.3 2.8 fusion.138
  591.1 3.2 fusion.139
  594.5 3.9 fusion.141
  599.4 1.7 fusion.75
  (199 shorter events, 30.7 us)
Async XLA Ops:
  7.2 90.1 %copy-start = (bf16[1024,1024]{1,0:T(8,128)(2,1)S(1)}, bf16[1024,1024]{1,0:T(8,128)(2,1)}, u32[]{:S(2)}) copy-start(bf16[1024,1024]{1,0:T(8,128)(2,1)} %param.22) | copy-start | bytes 6291460
  7.2 42.2 %all-gather.5.cloned.1.call-start = ((), (), s32[]{:S(2)}) async-start(), calls=%async_computation | async-start | bytes 4718592 | tf_op jit(solution)/shard_map/all_gather | solution.py:145
  7.9 344.9 %all-gather.7.cloned.1.call-start = ((), (), s32[]{:S(2)}) async-start(), calls=%async_computation.1 | async-start | bytes 20971520 | tf_op jit(solution)/shard_map/all_gather | solution.py:146
  49.4 338.6 %all-gather.9.cloned.1.call-start = ((), (), s32[]{:S(2)}) async-start(), calls=%async_computation.2 | async-start | bytes 4718592 | tf_op jit(solution)/shard_map/all_gather | solution.py:161
  50.1 502.6 %all-gather.11.cloned.1.call-start = ((), (), s32[]{:S(2)}) async-start(), calls=%async_computation.3 | async-start | bytes 37748736 | tf_op jit(solution)/shard_map/all_gather | solution.py:157
  50.7 48.1 %collective-permute-start.3 = (bf16[1024,256]{1,0:T(8,128)(2,1)S(1)}, bf16[1024,256]{1,0:T(8,128)(2,1)}, u32[]{:S(2)}, u32[]{:S(2)}) collective-permute-start(bf16[1024,256]{1,0:T(8,128)(2,1)S(1)} %copy-done.4), channel_id=1, source_target_pairs={{0,4},{4,8},{8,12},{12,16},{16,20},{20,24},{24,28},{28,0},{1,5},{5... | collective-permute-start | bytes 1572872 | tf_op jit(solution)/shard_map/ppermute | solution.py:21
  51.0 77.4 %collective-permute-start.7 = (bf16[1024,256]{1,0:T(8,128)(2,1)S(1)}, bf16[1024,256]{1,0:T(8,128)(2,1)S(1)}, u32[]{:S(2)}, u32[]{:S(2)}) collective-permute-start(bf16[1024,256]{1,0:T(8,128)(2,1)S(1)} %copy-done.4), channel_id=1, source_target_pairs={{0,28},{4,0},{8,4},{12,8},{16,12},{20,16},{24,20},{28,24},{1,29},{... | collective-permute-start | bytes 1572872 | tf_op jit(solution)/shard_map/ppermute | solution.py:23
  58.6 16.0 %collective-permute-start.1 = (bf16[128,1024]{1,0:T(8,128)(2,1)}, bf16[128,1024]{1,0:T(8,128)(2,1)}, u32[]{:S(2)}, u32[]{:S(2)}) collective-permute-start(bf16[128,1024]{1,0:T(8,128)(2,1)} %get-tuple-element.316), channel_id=1, source_target_pairs={{0,1},{1,2},{2,3},{3,4},{4,5},{5,6},{6,7},{7,8},{8,9},{9,10},{10,1... | collective-permute-start | bytes 786440 | tf_op jit(solution)/shard_map/ppermute | solution.py:31
  62.7 21.1 %collective-permute-start = (bf16[128,1024]{1,0:T(8,128)(2,1)}, bf16[128,1024]{1,0:T(8,128)(2,1)}, u32[]{:S(2)}, u32[]{:S(2)}) collective-permute-start(bf16[128,1024]{1,0:T(8,128)(2,1)} %get-tuple-element.318), channel_id=1, source_target_pairs={{0,1},{1,2},{2,3},{3,4},{4,5},{5,6},{6,7},{7,8},{8,9},{9,10},{10,1... | collective-permute-start | bytes 786440 | tf_op jit(solution)/shard_map/ppermute | solution.py:31
  71.5 40.7 %copy-start.47 = (pred[128]{0:T(512)(128)(4,1)}, pred[128]{0:T(512)(128)(4,1)S(1)}, u32[]{:S(2)}) copy-start(pred[128]{0:T(512)(128)(4,1)S(1)} %subtract_compare_fusion.1) | copy-start | bytes 388
  98.8 9.8 %collective-permute-start.4 = (bf16[1024,256]{1,0:T(8,128)(2,1)}, bf16[1024,256]{1,0:T(8,128)(2,1)S(1)}, u32[]{:S(2)}, u32[]{:S(2)}) collective-permute-start(bf16[1024,256]{1,0:T(8,128)(2,1)} %collective-permute-done.3), channel_id=1, source_target_pairs={{0,4},{4,8},{8,12},{12,16},{16,20},{20,24},{24,28},{28,0},{1,5},{5... | collective-permute-start | bytes 1572872 | tf_op jit(solution)/shard_map/ppermute | solution.py:21
  101.5 29.7 %copy-start.15 = (f32[1,1024]{1,0:T(1,128)S(1)}, f32[1,1024]{1,0:T(1,128)}, u32[]{:S(2)}) copy-start(f32[1,1024]{1,0:T(1,128)} %get-tuple-element.340) | copy-start | bytes 12292
  101.5 29.7 %copy-start.16 = (f32[1,1024]{1,0:T(1,128)S(1)}, f32[1,1024]{1,0:T(1,128)}, u32[]{:S(2)}) copy-start(f32[1,1024]{1,0:T(1,128)} %get-tuple-element.341) | copy-start | bytes 12292
  101.5 29.7 %copy-start.17 = (f32[1,1024]{1,0:T(1,128)S(1)}, f32[1,1024]{1,0:T(1,128)}, u32[]{:S(2)}) copy-start(f32[1,1024]{1,0:T(1,128)} %get-tuple-element.342) | copy-start | bytes 12292
  101.5 29.7 %copy-start.18 = (f32[1,1024]{1,0:T(1,128)S(1)}, f32[1,1024]{1,0:T(1,128)}, u32[]{:S(2)}) copy-start(f32[1,1024]{1,0:T(1,128)} %get-tuple-element.343) | copy-start | bytes 12292
  101.5 29.6 %copy-start.19 = (f32[1,1024]{1,0:T(1,128)S(1)}, f32[1,1024]{1,0:T(1,128)}, u32[]{:S(2)}) copy-start(f32[1,1024]{1,0:T(1,128)} %get-tuple-element.344) | copy-start | bytes 12292
  101.5 29.6 %copy-start.20 = (f32[1,1024]{1,0:T(1,128)S(1)}, f32[1,1024]{1,0:T(1,128)}, u32[]{:S(2)}) copy-start(f32[1,1024]{1,0:T(1,128)} %get-tuple-element.345) | copy-start | bytes 12292
  101.5 29.6 %copy-start.21 = (f32[1,1024]{1,0:T(1,128)S(1)}, f32[1,1024]{1,0:T(1,128)}, u32[]{:S(2)}) copy-start(f32[1,1024]{1,0:T(1,128)} %get-tuple-element.346) | copy-start | bytes 12292
  101.6 29.6 %copy-start.22 = (f32[1,1024]{1,0:T(1,128)S(1)}, f32[1,1024]{1,0:T(1,128)}, u32[]{:S(2)}) copy-start(f32[1,1024]{1,0:T(1,128)} %get-tuple-element.347) | copy-start | bytes 12292
  101.6 29.6 %copy-start.23 = (f32[1,1024]{1,0:T(1,128)S(1)}, f32[1,1024]{1,0:T(1,128)}, u32[]{:S(2)}) copy-start(f32[1,1024]{1,0:T(1,128)} %get-tuple-element.348) | copy-start | bytes 12292
  101.6 29.6 %copy-start.24 = (f32[1,1024]{1,0:T(1,128)S(1)}, f32[1,1024]{1,0:T(1,128)}, u32[]{:S(2)}) copy-start(f32[1,1024]{1,0:T(1,128)} %get-tuple-element.349) | copy-start | bytes 12292
  101.6 29.6 %copy-start.25 = (f32[1,1024]{1,0:T(1,128)S(1)}, f32[1,1024]{1,0:T(1,128)}, u32[]{:S(2)}) copy-start(f32[1,1024]{1,0:T(1,128)} %get-tuple-element.350) | copy-start | bytes 12292
  101.6 29.6 %copy-start.26 = (f32[1,1024]{1,0:T(1,128)S(1)}, f32[1,1024]{1,0:T(1,128)}, u32[]{:S(2)}) copy-start(f32[1,1024]{1,0:T(1,128)} %get-tuple-element.351) | copy-start | bytes 12292
  101.6 29.6 %copy-start.27 = (f32[1,1024]{1,0:T(1,128)S(1)}, f32[1,1024]{1,0:T(1,128)}, u32[]{:S(2)}) copy-start(f32[1,1024]{1,0:T(1,128)} %get-tuple-element.321) | copy-start | bytes 12292
  101.6 29.6 %copy-start.28 = (f32[1,1024]{1,0:T(1,128)S(1)}, f32[1,1024]{1,0:T(1,128)}, u32[]{:S(2)}) copy-start(f32[1,1024]{1,0:T(1,128)} %get-tuple-element.322) | copy-start | bytes 12292
  101.6 29.6 %copy-start.29 = (f32[1,1024]{1,0:T(1,128)S(1)}, f32[1,1024]{1,0:T(1,128)}, u32[]{:S(2)}) copy-start(f32[1,1024]{1,0:T(1,128)} %get-tuple-element.323) | copy-start | bytes 12292
  101.6 29.6 %copy-start.30 = (f32[1,1024]{1,0:T(1,128)S(1)}, f32[1,1024]{1,0:T(1,128)}, u32[]{:S(2)}) copy-start(f32[1,1024]{1,0:T(1,128)} %get-tuple-element.324) | copy-start | bytes 12292
  101.6 29.6 %copy-start.31 = (f32[1,1024]{1,0:T(1,128)S(1)}, f32[1,1024]{1,0:T(1,128)}, u32[]{:S(2)}) copy-start(f32[1,1024]{1,0:T(1,128)} %get-tuple-element.325) | copy-start | bytes 12292
  101.7 29.6 %copy-start.32 = (f32[1,1024]{1,0:T(1,128)S(1)}, f32[1,1024]{1,0:T(1,128)}, u32[]{:S(2)}) copy-start(f32[1,1024]{1,0:T(1,128)} %get-tuple-element.326) | copy-start | bytes 12292
  101.7 29.6 %copy-start.33 = (f32[1,1024]{1,0:T(1,128)S(1)}, f32[1,1024]{1,0:T(1,128)}, u32[]{:S(2)}) copy-start(f32[1,1024]{1,0:T(1,128)} %get-tuple-element.327) | copy-start | bytes 12292
  101.7 29.6 %copy-start.34 = (f32[1,1024]{1,0:T(1,128)S(1)}, f32[1,1024]{1,0:T(1,128)}, u32[]{:S(2)}) copy-start(f32[1,1024]{1,0:T(1,128)} %get-tuple-element.328) | copy-start | bytes 12292
  101.7 29.6 %copy-start.35 = (f32[1,1024]{1,0:T(1,128)S(1)}, f32[1,1024]{1,0:T(1,128)}, u32[]{:S(2)}) copy-start(f32[1,1024]{1,0:T(1,128)} %get-tuple-element.329) | copy-start | bytes 12292
  101.7 29.6 %copy-start.36 = (f32[1,1024]{1,0:T(1,128)S(1)}, f32[1,1024]{1,0:T(1,128)}, u32[]{:S(2)}) copy-start(f32[1,1024]{1,0:T(1,128)} %get-tuple-element.330) | copy-start | bytes 12292
  101.7 29.6 %copy-start.37 = (f32[1,1024]{1,0:T(1,128)S(1)}, f32[1,1024]{1,0:T(1,128)}, u32[]{:S(2)}) copy-start(f32[1,1024]{1,0:T(1,128)} %get-tuple-element.331) | copy-start | bytes 12292
  101.7 29.6 %copy-start.38 = (f32[1,1024]{1,0:T(1,128)S(1)}, f32[1,1024]{1,0:T(1,128)}, u32[]{:S(2)}) copy-start(f32[1,1024]{1,0:T(1,128)} %get-tuple-element.332) | copy-start | bytes 12292
  101.7 29.6 %copy-start.39 = (f32[1,1024]{1,0:T(1,128)S(1)}, f32[1,1024]{1,0:T(1,128)}, u32[]{:S(2)}) copy-start(f32[1,1024]{1,0:T(1,128)} %get-tuple-element.333) | copy-start | bytes 12292
  101.7 29.6 %copy-start.40 = (f32[1,1024]{1,0:T(1,128)S(1)}, f32[1,1024]{1,0:T(1,128)}, u32[]{:S(2)}) copy-start(f32[1,1024]{1,0:T(1,128)} %get-tuple-element.334) | copy-start | bytes 12292
  101.7 29.6 %copy-start.41 = (f32[1,1024]{1,0:T(1,128)S(1)}, f32[1,1024]{1,0:T(1,128)}, u32[]{:S(2)}) copy-start(f32[1,1024]{1,0:T(1,128)} %get-tuple-element.335) | copy-start | bytes 12292
  101.8 29.6 %copy-start.42 = (f32[1,1024]{1,0:T(1,128)S(1)}, f32[1,1024]{1,0:T(1,128)}, u32[]{:S(2)}) copy-start(f32[1,1024]{1,0:T(1,128)} %get-tuple-element.336) | copy-start | bytes 12292
  101.8 29.6 %copy-start.43 = (f32[1,1024]{1,0:T(1,128)S(1)}, f32[1,1024]{1,0:T(1,128)}, u32[]{:S(2)}) copy-start(f32[1,1024]{1,0:T(1,128)} %get-tuple-element.337) | copy-start | bytes 12292
  101.8 29.6 %copy-start.44 = (f32[1,1024]{1,0:T(1,128)S(1)}, f32[1,1024]{1,0:T(1,128)}, u32[]{:S(2)}) copy-start(f32[1,1024]{1,0:T(1,128)} %get-tuple-element.338) | copy-start | bytes 12292
  101.8 29.6 %copy-start.45 = (f32[1,1024]{1,0:T(1,128)S(1)}, f32[1,1024]{1,0:T(1,128)}, u32[]{:S(2)}) copy-start(f32[1,1024]{1,0:T(1,128)} %get-tuple-element.339) | copy-start | bytes 12292
  108.6 21.8 %collective-permute-start.5 = (bf16[1024,256]{1,0:T(8,128)(2,1)S(1)}, bf16[1024,256]{1,0:T(8,128)(2,1)S(1)}, u32[]{:S(2)}, u32[]{:S(2)}) collective-permute-start(bf16[1024,256]{1,0:T(8,128)(2,1)S(1)} %collective-permute-done.4), channel_id=1, source_target_pairs={{0,4},{4,8},{8,12},{12,16},{16,20},{20,24},{24,28},{28,0},{1,5},{5... | collective-permute-start | bytes 1572872 | tf_op jit(solution)/shard_map/ppermute | solution.py:21
  112.4 16.0 %collective-permute-start.2 = (bf16[30,1024]{1,0:T(8,128)(2,1)S(1)}, bf16[30,1024]{1,0:T(8,128)(2,1)S(1)}, u32[]{:S(2)}, u32[]{:S(2)}) collective-permute-start(bf16[30,1024]{1,0:T(8,128)(2,1)S(1)} %slice.294), channel_id=1, source_target_pairs={{0,1},{1,2},{2,3},{3,4},{4,5},{5,6},{6,7},{7,8},{8,9},{9,10},{10,1... | collective-permute-start | bytes 184328 | tf_op jit(solution)/shard_map/ppermute | solution.py:31
  128.4 44.8 %collective-permute-start.8 = (bf16[1024,256]{1,0:T(8,128)(2,1)S(1)}, bf16[1024,256]{1,0:T(8,128)(2,1)S(1)}, u32[]{:S(2)}, u32[]{:S(2)}) collective-permute-start(bf16[1024,256]{1,0:T(8,128)(2,1)S(1)} %collective-permute-done.7), channel_id=1, source_target_pairs={{0,28},{4,0},{8,4},{12,8},{16,12},{20,16},{24,20},{28,24},{1,29},{... | collective-permute-start | bytes 1572872 | tf_op jit(solution)/shard_map/ppermute | solution.py:23
  130.4 42.8 %collective-permute-start.6 = (bf16[1024,256]{1,0:T(8,128)(2,1)S(1)}, bf16[1024,256]{1,0:T(8,128)(2,1)S(1)}, u32[]{:S(2)}, u32[]{:S(2)}) collective-permute-start(bf16[1024,256]{1,0:T(8,128)(2,1)S(1)} %collective-permute-done.5), channel_id=1, source_target_pairs={{0,4},{4,8},{8,12},{12,16},{16,20},{20,24},{24,28},{28,0},{1,5},{5... | collective-permute-start | bytes 1572872 | tf_op jit(solution)/shard_map/ppermute | solution.py:21
  173.2 7.0 %collective-permute-start.9 = (bf16[1024,256]{1,0:T(8,128)(2,1)S(1)}, bf16[1024,256]{1,0:T(8,128)(2,1)S(1)}, u32[]{:S(2)}, u32[]{:S(2)}) collective-permute-start(bf16[1024,256]{1,0:T(8,128)(2,1)S(1)} %collective-permute-done.8), channel_id=1, source_target_pairs={{0,28},{4,0},{8,4},{12,8},{16,12},{20,16},{24,20},{28,24},{1,29},{... | collective-permute-start | bytes 1572872 | tf_op jit(solution)/shard_map/ppermute | solution.py:23
  188.8 172.4 %copy-start.12 = (f32[8192]{0:T(1024)S(1)}, f32[8192]{0:T(1024)}, u32[]{:S(2)}) copy-start(f32[8192]{0:T(1024)} %param.28) | copy-start | bytes 98308
  (17 other events, 167.5 us)
Sparse Core Ops, SparseCore 0:
  9.9 39.4 all-gather.4
  50.9 301.8 all-gather.6
  354.7 33.2 all-gather.8
  389.8 162.8 all-gather.10
